TPU v7x, 32 devices: a whole 2x2x4 slice. The times are simulated.
32 devices in a mesh: groups: 2 (over y), seq: 4 (over z), head: 2 (over x), rep: 2 (over core).
Axes of the slice: x: 2, y: 2, z: 4, core: 2. Of those that a mesh axis runs over, the one named last changes fastest.
Arguments:
- document_query: bfloat16 [4096, 8192], P(('groups', 'seq', 'rep'), 'head'), parts along dimension 0, may hold values from -6 to 6
- document_key: bfloat16 [4096, 8192], P(('groups', 'seq', 'rep'), 'head'), parts along dimension 0, may hold values from -0.059814453 to 0.059814453
- document_value: bfloat16 [4096, 8192], P(('groups', 'seq', 'rep'), 'head'), parts along dimension 0, may hold values from -6 to 6
- document_decay: float32 [4096, 64], P(('groups', 'seq', 'rep'), 'head'), parts along dimension 0, may hold values from 0 to 1, as said below
- passage_query: bfloat16 [16, 256, 8192], P(('groups', 'seq', 'rep'), None, 'head'), parts along dimension 0, may hold values from -6 to 6
- passage_key: bfloat16 [16, 256, 8192], P(('groups', 'seq', 'rep'), None, 'head'), parts along dimension 0, may hold values from -0.059814453 to 0.059814453
- passage_value: bfloat16 [16, 256, 8192], P(('groups', 'seq', 'rep'), None, 'head'), parts along dimension 0, may hold values from -6 to 6
- passage_gate: bfloat16 [16, 256, 8192], P(('groups', 'seq', 'rep'), None, 'head'), parts along dimension 0, may hold values from -8 to 8
- passage_decay: float32 [16, 256, 64], P(('groups', 'seq', 'rep'), None, 'head'), parts along dimension 0, may hold values from 0 to 1, as said below
- passage_length: int32 [16], P(('groups', 'seq', 'rep')), parts along dimension 0, may hold values from 64 to 256, as said below
- norm_gain: float32 [8192], P('head'), may hold values from 0.1 to 1.9
Outputs:
- document_output: bfloat16 [4096, 8192], P(('groups', 'seq', 'rep'), 'head'), parts along dimension 0
- passage_output: bfloat16 [16, 256, 8192], P(('groups', 'seq', 'rep'), None, 'head'), parts along dimension 0
There are 2 independent parts, one for each index of `groups`. A program takes and returns all parts, laid end to end along the dimension named above; an argument that names none is the same for every part. Nothing has to cross between parts.
Inputs may be any that keep to these rules, and one draw needn't show every extreme that they name: `document_decay`: positive per-position log-decay rates. `passage_decay`: positive per-position log-decay rates. `passage_length`: a passage's valid tokens are its first ones.
All inputs are finite; a program needn't handle non-finite values.
Results may differ from a plain program's by a relative error of at most 0.0046.
Values sent between devices are 32-bit elements; how exact they have to be, the bound alone decides.
A program may use at most 128 MiB of HBM per device.

v0:
```python
import jax
import jax.numpy as jnp
from jax import lax
from jax.sharding import PartitionSpec as P

epsilon = 1e-05


def entering_2(value, axis, combine, identity, reverse):
    peers, place = (lax.axis_size(axis), lax.axis_index(axis))
    everything = jax.tree.map(lambda part: lax.all_gather(part, axis), value)
    start = jax.tree.map(
        lambda part, zero: jnp.broadcast_to(jnp.asarray(zero, part.dtype), part.shape),
        value,
        identity,
    )

    def hop(k, before):
        at = peers - 1 - k if reverse else k
        reached = at > place if reverse else at < place
        new = combine(before, jax.tree.map(lambda part: part[at], everything))
        return jax.tree.map(lambda a, b: jnp.where(reached, a, b), new, before)

    return lax.fori_loop(0, peers, hop, start)


def local_block(queries, keys_in, values_in, rates):
    length = queries.shape[0]
    cumulative = jnp.cumsum(rates, axis=0)
    scores = jnp.einsum("thd,shd->hts", queries, keys_in, preferred_element_type=jnp.float32)
    ordered = jnp.transpose(cumulative)
    spread = ordered[:, None, :] - ordered[:, :, None]
    causal = (
        lax.broadcasted_iota(jnp.int32, (length, length), 0)
        >= lax.broadcasted_iota(jnp.int32, (length, length), 1)
    )[None]
    weights = jnp.where(causal, scores * jnp.exp(jnp.where(causal, spread, 0.0)), 0.0).astype(
        jnp.bfloat16
    )
    intra_part = jnp.einsum("hts,shd->thd", weights, values_in, preferred_element_type=jnp.float32)
    return (intra_part, cumulative)


def carried(queries, cumulative, state_full):
    inter_part = jnp.einsum(
        "thd,hde->the", queries.astype(jnp.float32), state_full, precision=lax.Precision.HIGHEST
    )
    return inter_part * jnp.exp(-cumulative)[:, :, None]


def block_state(keys_in, values_in, cumulative):
    closing = cumulative[-1]
    scaled_key = (
        keys_in.astype(jnp.float32) * jnp.exp(cumulative - closing[None, :])[:, :, None]
    ).astype(jnp.bfloat16)
    state = jnp.einsum("shd,she->hde", scaled_key, values_in, preferred_element_type=jnp.float32)
    return (state, jnp.exp(-closing))


def chain_step(earlier, later):
    return (earlier[0] * later[0], later[0][:, None, None] * earlier[1] + later[1])


def multiply(earlier, later):
    return earlier * later


def local(
    document_query,
    document_key,
    document_value,
    document_decay,
    passage_query,
    passage_key,
    passage_value,
    passage_gate,
    passage_decay,
    passage_length,
    norm_gain,
):
    heads_here = document_decay.shape[1]
    head_dim = document_query.shape[1] // heads_here
    doc_rows = document_query.shape[0]
    passage_count = passage_query.shape[0]
    passage_rows = passage_query.shape[1]
    doc_queries = document_query.reshape(doc_rows, heads_here, head_dim)
    doc_keys = document_key.reshape(doc_rows, heads_here, head_dim)
    doc_values = document_value.reshape(doc_rows, heads_here, head_dim)
    intra_doc, cumulative = local_block(doc_queries, doc_keys, doc_values, document_decay)
    state_own, decay_own = block_state(doc_keys, doc_values, cumulative)
    decay_before, entering = entering_2(
        (decay_own, state_own),
        ("seq", "rep"),
        chain_step,
        (jnp.ones_like(decay_own), jnp.zeros_like(state_own)),
        False,
    )
    document_output = (intra_doc + carried(doc_queries, cumulative, entering)).astype(jnp.bfloat16)
    document_output = document_output.reshape(doc_rows, heads_here * head_dim)
    decay_after = entering_2(decay_own, ("seq", "rep"), multiply, jnp.ones_like(decay_own), True)
    memory = lax.psum(decay_after[:, None, None] * state_own, ("seq", "rep"))

    def readout(inputs):
        queries, keys_in, values_in, rates = inputs
        queries = queries.reshape(passage_rows, heads_here, head_dim)
        intra_part, running = local_block(
            queries,
            keys_in.reshape(passage_rows, heads_here, head_dim),
            values_in.reshape(passage_rows, heads_here, head_dim),
            rates,
        )
        attended = (intra_part + carried(queries, running, memory)).reshape(
            passage_rows, heads_here * head_dim
        )
        return (attended, jnp.sum(attended * attended, axis=1))

    attended, squares = lax.map(readout, (passage_query, passage_key, passage_value, passage_decay))
    totals = lax.psum(squares, "head")
    features_all = attended.shape[-1] * lax.axis_size("head")
    scaling = lax.rsqrt(totals / features_all + epsilon)
    normed = (
        attended
        * scaling[:, :, None]
        * norm_gain[None, None, :]
        * jax.nn.sigmoid(passage_gate.astype(jnp.float32))
    )
    inside = (
        lax.broadcasted_iota(jnp.int32, (passage_count, passage_rows), 1) < passage_length[:, None]
    )
    passage_output = jnp.where(inside[:, :, None], normed, 0.0).astype(jnp.bfloat16)
    return (document_output, passage_output)


def solution(mesh):
    in_specs = (
        P(("groups", "seq", "rep"), "head"),
        P(("groups", "seq", "rep"), "head"),
        P(("groups", "seq", "rep"), "head"),
        P(("groups", "seq", "rep"), "head"),
        P(("groups", "seq", "rep"), None, "head"),
        P(("groups", "seq", "rep"), None, "head"),
        P(("groups", "seq", "rep"), None, "head"),
        P(("groups", "seq", "rep"), None, "head"),
        P(("groups", "seq", "rep"), None, "head"),
        P(("groups", "seq", "rep")),
        P("head"),
    )
    out_specs = (P(("groups", "seq", "rep"), "head"), P(("groups", "seq", "rep"), None, "head"))
    return jax.shard_map(local, mesh=mesh, in_specs=in_specs, out_specs=out_specs, check_vma=False)
```

profile of v0, /device:TPU:0, one launch (start us, length us, event | category | flops | bytes accessed | tf_op | source)
XLA Modules:
  0.0 281.8 jit_solution(3076644146216741903)
XLA Ops:
  7.2 0.0 copy-start
  7.2 0.0 all-reduce.2.cloned.1.call-start
  7.2 0.9 copy_bitcast_fusion.3
  8.1 0.6 reduce-window.14
  8.7 0.2 slice_reduce_fusion.1
  8.9 0.1 fusion.37
  9.0 0.2 slice_reduce_fusion.2
  9.2 0.1 negate_exponential_fusion
  9.3 13.5 %all-gather.1 = f32[8,1,32]{2,1,0:T(1,128)S(1)} all-gather(f32[1,1,32]{2,1,0:T(1,128)S(1)} %bitcast.131), channel_id=1, replica_groups=mesh['groups'=2,'seq'=4,'head'=2,'rep'=2] {'seq','rep'}, dimensions={0}, use_global_device_ids=true | all-gather | bytes 1152 | tf_op jit(solution)/shard_map/all_gather | solution.py:11
  22.8 0.3 while.36
  23.1 4.1 %copy.82 = bf16[256,4096]{0,1:T(8,128)(2,1)} copy(bf16[256,4096]{1,0:T(8,128)(2,1)} %param.16) | data formatting | bytes 4194304 | tf_op jit(solution)/shard_map/reshape | solution.py:87
  27.1 0.0 copy-done
  27.1 4.4 %broadcast_multiply_fusion = (f32[32,128,128]{2,1,0:T(8,128)}, f32[32,128,128]{2,1,0:T(8,128)}) fusion(f32[32]{0:T(128)S(1)} %get-tuple-element.231, bf16[256,32,128]{0,2,1:T(8,128)(2,1)} %bitcast.121, f32[256,32]{0,1:T(8,128)S(1)} %get-tuple-element.294, bf16[256,4096]{1,0:T(8,128)(2,1)S(1)} %copy-done), kind=kOutput, calls=%fused_computation.40 | convolution fusion | flops 272105472 | bytes 8421504 | tf_op jit(solution)/shard_map/shd,she->hde/dot_general | solution.py:56
  31.5 0.0 copy-start.4
  31.5 0.0 all-reduce.2.cloned.1.call-update
  31.6 0.0 all-gather.4.cloned.1.call-start
  31.6 0.7 all-gather.4.cloned.1.call-update
  32.3 0.0 copy-done.4
  32.3 0.6 reduce-window.16
  32.9 0.2 slice_reduce_fusion
  33.1 3.4 %copy.89 = bf16[32,8,32,128]{3,2,1,0:T(8,128)(2,1)} copy(bf16[32,8,32,128]{3,1,2,0:T(8,128)(2,1)} %bitcast.124) | data formatting | bytes 4194304
  36.5 4.1 %copy.81 = bf16[1,256,4096]{1,2,0:T(8,128)(2,1)} copy(bf16[1,256,4096]{2,1,0:T(8,128)(2,1)} %param.21) | data formatting | bytes 4194304 | tf_op jit(solution)/shard_map/while/body/eval_jaxpr/reshape | solution.py:109
  40.6 3.5 %copy.90 = bf16[32,8,32,128]{3,2,1,0:T(8,128)(2,1)} copy(bf16[32,8,32,128]{3,1,2,0:T(8,128)(2,1)} %bitcast.125) | data formatting | bytes 4194304
  44.8 0.1 copy_bitcast_fusion
  44.9 0.1 exponential_bitcast_fusion
  45.0 6.4 %fusion.1 = f32[32,256,128]{1,2,0:T(8,128)} fusion(f32[32,256]{1,0:T(8,128)S(1)} %get-tuple-element.296, pred[256,256]{1,0:T(8,128)(4,1)S(1)} %iota_compare_fusion, bf16[256,32,128]{0,2,1:T(8,128)(2,1)} %bitcast.122, bf16[256,4096]{1,0:T(8,128)(2,1)S(1)} %copy-done, bf16[256,4096]{1,0:T(8,128)(2,1)} %param.15), kind=kOutput, calls=%fused_computation.7 | convolution fusion | flops 1084227584 | bytes 10584064 | tf_op jit(solution)/shard_map/hts,shd->thd/dot_general | solution.py:40
  51.3 0.0 copy-start.3
  51.3 7.3 %fusion.2 = f32[32,256,128]{1,2,0:T(8,128)} fusion(bf16[256,32,128]{0,2,1:T(8,128)(2,1)} %bitcast.126, f32[32,256]{1,0:T(8,128)S(1)} %copy_bitcast_fusion, pred[256,256]{1,0:T(8,128)(4,1)S(1)} %iota_compare_fusion, bf16[256,32,128]{2,1,0:T(8,128)(2,1)} %bitcast.127, bf16[256,32,128]{2,1,0:T(8,128)(2,1)} %bitcast.118), kind=kOutput, calls=%fused_computation.8 | convolution fusion | flops 1084227584 | bytes 10584064 | tf_op jit(solution)/shard_map/while/body/eval_jaxpr/hts,shd->thd/dot_general | solution.py:40
  58.7 36.5 %all-reduce.2.cloned.1.call-done = f32[32,128,128]{2,1,0:T(8,128)} async-done(((f32[32,128,128]{2,1,0:T(8,128)}), f32[32,128,128]{2,1,0:T(8,128)}) %all-reduce.2.cloned.1.call-update) | async-done | bytes 2097168 | tf_op jit(solution)/shard_map/psum | solution.py:101
  95.1 0.0 copy-done.3
  95.1 7.8 %multiply_reduce_fusion = (f32[256]{0:T(256)S(1)}, f32[256,32,128]{0,2,1:T(8,128)}) fusion(f32[256,32]{0,1:T(8,128)S(1)} %exponential_bitcast_fusion, f32[32,128,128]{2,1,0:T(8,128)} %all-reduce.2.cloned.1.call-done, bf16[256,32,128]{2,1,0:T(8,128)(2,1)S(1)} %bitcast.119, f32[32,256,128]{1,2,0:T(8,128)} %fusion.2), kind=kOutput, calls=%fused_computation.15 | convolution fusion | flops 1614806784 | bytes 12616704 | tf_op jit(solution)/shard_map/while/body/eval_jaxpr/thd,hde->the/dot_general | solution.py:45
  102.9 0.0 copy-start.5
  102.9 6.1 %copy.77 = f32[1,256,4096]{2,1,0:T(8,128)} copy(f32[1,256,4096]{1,2,0:T(8,128)} %bitcast.117) | data formatting | bytes 8388608 | tf_op jit(solution)/shard_map/while/body/jit(dynamic_update_index_in_dim)/broadcast_in_dim | solution.py:117
  108.9 5.1 %psum.15 = f32[1,256]{1,0:T(1,128)S(1)} all-reduce(f32[1,256]{1,0:T(1,128)S(1)} %bitcast.129), channel_id=1, replica_groups=mesh['groups'=2,'seq'=4,'head'=2,'rep'=2] {'head'}, use_global_device_ids=true, to_apply=%region_10.11 | all-reduce | flops 256 | bytes 2048 | tf_op jit(solution)/shard_map/psum | solution.py:118
  114.0 0.0 copy-done.5
  114.0 0.0 copy-start.2
  114.0 5.9 %select_convert_fusion.4 = bf16[1,256,4096]{2,1,0:T(8,128)(2,1)} fusion(bf16[1,256,4096]{2,1,0:T(8,128)(2,1)} %param.22, f32[1,256,4096]{2,1,0:T(8,128)} %copy.77, f32[4096]{0:T(1024)S(1)} %copy-done.5, f32[256]{0:T(256)S(1)} %bitcast.130, pred[256]{0:T(512)(128)(4,1)S(1)} %iota_compare_fusion.1), kind=kLoop, calls=%fused_computation.14 | loop fusion | flops 9437184 | bytes 8406272 | tf_op jit(solution)/shard_map/convert_element_type | solution.py:130
  119.9 127.5 %all-gather.4.cloned.1.call-done = f32[256,128,128]{2,1,0:T(8,128)} async-done(((f32[32,128,128]{2,1,0:T(8,128)}), f32[256,128,128]{2,1,0:T(8,128)}) %all-gather.4.cloned.1.call-update) | async-done | bytes 16777232 | tf_op jit(solution)/shard_map/all_gather | solution.py:11
  247.4 0.0 copy-done.2
  247.4 17.0 %while.35 = (s32[]{:T(128)}, f32[32,128,128]{2,1,0:T(8,128)S(1)}, s32[]{:T(128)}, f32[8,32]{1,0:T(8,128)S(1)}, f32[8,32,128,128]{3,2,1,0:T(8,128)}, /*index=5*/s32[]{:T(128)}, s32[]{:T(128)}) while((s32[]{:T(128)}, f32[32,128,128]{2,1,0:T(8,128)S(1)}, s32[]{:T(128)}, f32[8,32]{1,0:T(8,128)S(1)}, f32[8,32,128,128]{3,2,1,0:T(8,128)}, ...), condition=%wide.region_3.4_spmd.clone, body=%wide.region_2.3_spmd.clone.sunk | while | flops 2097156 | bytes 6291945 | solution.py:24
  247.4 2.1 fusion.49
  249.6 2.1 fusion.49
  251.7 2.1 fusion.49
  253.8 2.1 fusion.49
  256.0 2.1 fusion.49
  258.1 2.1 fusion.49
  260.2 2.1 fusion.49
  262.4 2.1 fusion.49
  264.5 6.3 %fusion.5 = bf16[256,32,128]{0,2,1:T(8,128)(2,1)} fusion(f32[32,256,128]{1,2,0:T(8,128)} %fusion.1, f32[32,128,128]{2,1,0:T(8,128)S(1)} %get-tuple-element.230, f32[256,32]{0,1:T(8,128)S(1)} %get-tuple-element.293, bf16[256,4096]{1,0:T(8,128)(2,1)} %param.15), kind=kOutput, calls=%fused_computation.13 | convolution fusion | flops 1613758464 | bytes 10518528 | tf_op jit(solution)/shard_map/thd,hde->the/dot_general | solution.py:45
  270.8 0.0 copy-start.1
  270.8 4.2 %copy.78 = bf16[256,4096]{1,0:T(8,128)(2,1)} copy(bf16[256,4096]{0,1:T(8,128)(2,1)} %bitcast.120) | data formatting | bytes 4194304
  275.0 0.0 copy-done.1
  (26 shorter events, 0.3 us)
Async XLA Ops:
  7.2 20.0 %copy-start = (bf16[256,4096]{1,0:T(8,128)(2,1)S(1)}, bf16[256,4096]{1,0:T(8,128)(2,1)}, u32[]{:S(2)}) copy-start(bf16[256,4096]{1,0:T(8,128)(2,1)} %param.17) | copy-start | bytes 6291460
  7.2 87.9 %all-reduce.2.cloned.1.call-start = ((), (), s32[]{:S(2)}) async-start(), calls=%async_computation | async-start | bytes 4194304 | tf_op jit(solution)/shard_map/psum | solution.py:101
  31.5 0.8 copy-start.4
  31.6 215.9 %all-gather.4.cloned.1.call-start = ((), (), s32[]{:S(2)}) async-start(), calls=%async_computation.1 | async-start | bytes 18874368 | tf_op jit(solution)/shard_map/all_gather | solution.py:11
  51.3 43.8 %copy-start.3 = (bf16[32,8,32,128]{3,2,1,0:T(8,128)(2,1)S(1)}, bf16[32,8,32,128]{3,2,1,0:T(8,128)(2,1)}, u32[]{:S(2)}) copy-start(bf16[32,8,32,128]{3,2,1,0:T(8,128)(2,1)} %copy.89) | copy-start | bytes 6291460
  102.9 11.2 %copy-start.5 = (f32[4096]{0:T(1024)S(1)}, f32[4096]{0:T(1024)}, u32[]{:S(2)}) copy-start(f32[4096]{0:T(1024)} %param.25) | copy-start | bytes 49156
  114.0 133.4 %copy-start.2 = (f32[32,128,128]{2,1,0:T(8,128)S(1)}, f32[32,128,128]{2,1,0:T(8,128)}, u32[]{:S(2)}) copy-start(f32[32,128,128]{2,1,0:T(8,128)} %custom-call) | copy-start | bytes 6291460
  270.8 4.2 %copy-start.1 = (bf16[256,4096]{1,0:T(8,128)(2,1)S(1)}, bf16[256,4096]{1,0:T(8,128)(2,1)}, u32[]{:S(2)}) copy-start(bf16[256,4096]{1,0:T(8,128)(2,1)} %param.17) | copy-start | bytes 6291460
Sparse Core Ops, SparseCore 0:
  31.7 63.3 all-reduce.1
  96.7 150.6 all-gather.3
where the time goes:
time: 283 us; the launch traced here: 282 us
  waiting for transfers between devices  165 us (58%)
  matrix products  32.1 us (11%)
  local copies, waits for them, and re-layouts  26.6 us (9%)
  other arithmetic  24.6 us (9%)
  blocking collectives  18.6 us (7%)
  between operations  14.8 us (5%)
    all_gather x1, waiting for transfers between devices, entering_2(): everything = jax.tree.map(lambda part: lax.all_gather(part, axis), value)  128 us
    psum x1, waiting for transfers between devices, local(): memory = lax.psum(decay_after[:, None, None] * state_own, ('seq', 'rep'))  36.5 us
    select_n x16, other arithmetic, hop(): return jax.tree.map(lambda a, b: jnp.where(reached, a, b), new, before)  16.9 us
    dot_general x2, matrix products, carried(): jnp.einsum('thd,hde->the', queries.astype(jnp.float32), state_full, preci...  14 us
    dot_general x2, matrix products, local_block(): jnp.einsum('hts,shd->thd', weights, values_in, preferred_element_type=jnp...  13.7 us
    all_gather x1, blocking collectives, entering_2(): everything = jax.tree.map(lambda part: lax.all_gather(part, axis), value)  13.5 us
    unnamed x15, local copies, waits for them, and re-layouts  11.1 us
    broadcast_in_dim x1, local copies, waits for them, and re-layouts, local(): lax.map(readout, (passage_query, passage_key, passage_value, passage_decay))  6.07 us
  transfers between devices with their start and end apart: 2, of which 2 were waited for; matrix products, arithmetic and copies ran while one was open for 16% of the time, Pallas kernels for 0%

commit v1 on v0

v1 whole, which is shorter than its diff:
```python
import functools

import jax
import jax.numpy as jnp
from jax import lax
from jax.experimental import pallas as pl
from jax.experimental.pallas import tpu as pltpu
from jax.sharding import PartitionSpec as P

epsilon = 1e-05
LAG = 2
MESH = pl.DeviceIdType.MESH


def column(row, lanes):
    length = row.shape[1]
    parts = [
        jnp.transpose(jnp.broadcast_to(row[:, a : a + lanes], (lanes, lanes)))
        for a in range(0, length, lanes)
    ]
    return jnp.concatenate(parts, axis=0)


def exact_dot(queries, state):
    high = state.astype(jnp.bfloat16)
    low = (state - high.astype(jnp.float32)).astype(jnp.bfloat16)
    return jnp.dot(
        jnp.concatenate([queries, queries], axis=1),
        jnp.concatenate([high, low], axis=0),
        preferred_element_type=jnp.float32,
    )


def kernel(
    n,
    hn,
    heads,
    hd,
    q_hbm,
    k_hbm,
    v_hbm,
    decay_ref,
    pq_hbm,
    pk_hbm,
    pv_hbm,
    pg_hbm,
    pdecay_ref,
    plen_ref,
    gain_ref,
    out_hbm,
    pout_hbm,
    q,
    k,
    v,
    pq,
    pk,
    pv,
    pg,
    dob,
    pob,
    dintra,
    pintra,
    cum_t,
    pcum_t,
    closings,
    d0_t,
    d1_t,
    dsuf_t,
    s_out,
    s_own,
    s_in,
    s_first,
    s_chip,
    f_in,
    f_out,
    b_in,
    b_out,
    e_own,
    e_out,
    e_in,
    m_out,
    m_in,
    acc,
    sq,
    scale,
    load_sem,
    store_sem,
    close_send,
    close_recv,
    pair_send,
    pair_recv,
    line_send,
    line_recv,
    sq_send,
    sq_recv,
):
    c, r, hx = lax.axis_index("seq"), lax.axis_index("rep"), lax.axis_index("head")
    rows = q.shape[0]
    prow = pq.shape[0]
    count = heads // 2
    blocks = 2 * n
    b = c * 2 + r
    f32 = jnp.float32
    high = lax.Precision.HIGHEST

    loads = [
        pltpu.make_async_copy(src, dst, load_sem.at[i])
        for i, (src, dst) in enumerate(
            [
                (k_hbm, k),
                (v_hbm, v),
                (q_hbm, q),
                (pk_hbm, pk),
                (pq_hbm, pq),
                (pv_hbm, pv),
                (pg_hbm, pg),
            ]
        )
    ]
    for load in loads:
        load.start()

    barrier = pltpu.get_barrier_semaphore()
    line = []
    for step in range(1, blocks):
        to = lax.rem(b + step, blocks)
        line.append({"seq": to // 2, "rep": lax.rem(to, 2)})
    across = [{"head": lax.rem(hx + step, hn)} for step in range(1, hn)]
    for peer in line + across:
        pl.semaphore_signal(barrier, inc=1, device_id=peer, device_id_type=MESH)

    def upper(length):
        return (
            lax.broadcasted_iota(jnp.int32, (length, length), 0)
            <= lax.broadcasted_iota(jnp.int32, (length, length), 1)
        ).astype(f32)

    contract_rows = (((0,), (0,)), ((), ()))
    contract_lanes = (((1,), (1,)), ((), ()))
    rates = decay_ref[...]
    sums = jnp.dot(jnp.ones((8, rows), f32), rates, precision=high, preferred_element_type=f32)
    closings[b] = jnp.zeros((1, hd), f32)
    closings[b, :, :heads] = sums[0:1]
    cum_t[...] = lax.dot_general(
        rates, upper(rows), contract_rows, precision=high, preferred_element_type=f32
    )
    pcum_t[...] = lax.dot_general(
        pdecay_ref[...], upper(prow), contract_rows, precision=high, preferred_element_type=f32
    )
    acc[...] = jnp.zeros_like(acc)

    @pl.when(c == 0)
    def _():
        f_in[...] = jnp.zeros_like(f_in)

    @pl.when(c == n - 1)
    def _():
        b_in[...] = jnp.zeros_like(b_in)

    pl.semaphore_wait(barrier, len(line) + len(across))

    close_copies = [
        pltpu.make_async_remote_copy(
            src_ref=closings.at[b],
            dst_ref=closings.at[b],
            send_sem=close_send.at[i],
            recv_sem=close_recv.at[i],
            device_id=peer,
            device_id_type=MESH,
        )
        for i, peer in enumerate(line)
    ]
    for copy in close_copies:
        copy.start()

    def pair_copy(kind, src, dst, j):
        return pltpu.make_async_remote_copy(
            src_ref=src.at[j],
            dst_ref=dst.at[j],
            send_sem=pair_send.at[kind, j],
            recv_sem=pair_recv.at[kind, j],
            device_id={"rep": 1 - r},
            device_id_type=MESH,
        )

    def line_copy(kind, src, dst, j, to):
        return pltpu.make_async_remote_copy(
            src_ref=src.at[j],
            dst_ref=dst.at[j],
            send_sem=line_send.at[kind, j],
            recv_sem=line_recv.at[kind, j],
            device_id={"seq": to},
            device_id_type=MESH,
        )

    def state_copy(j):
        return pair_copy(0, s_out, s_in, j)

    def entering_copy(j):
        return pair_copy(1, e_out, e_in, j)

    def memory_copy(j):
        return pair_copy(2, m_out, m_in, j)

    right, left = jnp.minimum(c + 1, n - 1), jnp.maximum(c - 1, 0)

    def forward_copy(j):
        return line_copy(0, f_out, f_in, j, right)

    def backward_copy(j):
        return line_copy(1, b_out, b_in, j, left)

    def lanes_of(h):
        return pl.ds(pl.multiple_of(h * hd, hd), hd)

    def own_head(j):
        return r * count + j

    def other_head(j):
        return (1 - r) * count + j

    def state_of(h):
        col = column(cum_t[pl.ds(h, 1), :], hd)
        scaled = (k[:, lanes_of(h)].astype(f32) * jnp.exp(col - col[rows - 1 : rows, :])).astype(
            jnp.bfloat16
        )
        return lax.dot_general(scaled, v[:, lanes_of(h)], contract_rows, preferred_element_type=f32)

    def intra(qs, ks, vs, cums, into, h):
        length = qs.shape[0]
        qh, kh, vh = qs[:, lanes_of(h)], ks[:, lanes_of(h)], vs[:, lanes_of(h)]
        row = cums[pl.ds(h, 1), :]
        col = column(row, hd)
        pieces = []
        for t in range(0, length, hd):
            ends = t + hd
            scores = lax.dot_general(
                qh[t:ends], kh[:ends], contract_lanes, preferred_element_type=f32
            )
            parts = []
            for s in range(0, ends, hd):
                part = scores[:, s : s + hd] * jnp.exp(row[:, s : s + hd] - col[t:ends])
                if s == t:
                    causal = lax.broadcasted_iota(jnp.int32, (hd, hd), 0) >= (
                        lax.broadcasted_iota(jnp.int32, (hd, hd), 1)
                    )
                    part = jnp.where(causal, part, 0.0)
                parts.append(part.astype(jnp.bfloat16))
            weights = jnp.concatenate(parts, axis=1)
            pieces.append(jnp.dot(weights, vh[:ends], preferred_element_type=f32))
        into[h] = jnp.concatenate(pieces, axis=0)

    def finish(h, entering, memory):
        grow = column(jnp.exp(-cum_t[pl.ds(h, 1), :]), hd)
        at = lanes_of(h)
        dob[:, at] = (dintra[h] + grow * exact_dot(q[:, at], entering)).astype(dob.dtype)
        pltpu.make_async_copy(dob.at[:, at], out_hbm.at[:, at], store_sem.at[0]).start()
        pgrow = column(jnp.exp(-pcum_t[pl.ds(h, 1), :]), hd)
        attended = pintra[h] + pgrow * exact_dot(pq[:, at], memory)
        acc[...] += attended * attended
        pintra[h] = attended * (gain_ref[:, at] * jax.nn.sigmoid(pg[:, at].astype(f32)))

    last = jnp.maximum(c, n - 1 - c) * LAG

    @pl.loop(0, count + (n - 1) * LAG + 2)
    def _(it):
        @pl.when(it == 0)
        def _():
            loads[0].wait()
            loads[1].wait()

        @pl.when(it == 1)
        def _():
            for copy in close_copies:
                copy.wait_recv()
            later = jnp.zeros((1, hd), f32)
            for at in range(2, blocks):
                later = later + jnp.where(at >= 2 * (c + 1), closings[at], 0.0)

            def table(values):
                return jnp.transpose(jnp.broadcast_to(jnp.exp(-values), (hd, hd)))

            d0_t[...] = table(closings[2 * c])
            d1_t[...] = table(closings[2 * c + 1])
            dsuf_t[...] = table(later)

        j0 = it - 1

        @pl.when((j0 >= 0) & (j0 < count))
        def _():
            state_copy(j0).wait_recv()
            one = jnp.where(r == 0, s_own[j0], s_in[j0])
            two = jnp.where(r == 0, s_in[j0], s_own[j0])
            s_first[j0] = one
            s_chip[j0] = d1_t[pl.ds(own_head(j0), 1), :] * one + two

        jf = it - 1 - c * LAG

        @pl.when((jf >= 0) & (jf < count))
        def _():
            h = own_head(jf)

            @pl.when(c > 0)
            def _():
                forward_copy(jf).wait_recv()

            before = f_in[jf]
            d0, d1 = d0_t[pl.ds(h, 1), :], d1_t[pl.ds(h, 1), :]
            f_out[jf] = (d0 * d1) * before + s_chip[jf]

            @pl.when(c < n - 1)
            def _():
                forward_copy(jf).start()

            second = d0 * before + s_first[jf]
            e_own[jf] = jnp.where(r == 0, before, second)
            e_out[jf] = jnp.where(r == 0, second, before)
            entering_copy(jf).start()

        jb = it - 1 - (n - 1 - c) * LAG

        @pl.when((jb >= 0) & (jb < count))
        def _():
            @pl.when(c < n - 1)
            def _():
                backward_copy(jb).wait_recv()

            @pl.when(c > 0)
            def _():
                b_out[jb] = dsuf_t[pl.ds(own_head(jb), 1), :] * s_chip[jb] + b_in[jb]
                backward_copy(jb).start()

        @pl.when(it < count)
        def _():
            s_out[it] = state_of(other_head(it))
            state_copy(it).start()
            s_own[it] = state_of(own_head(it))

        jm = it - 1 - last

        @pl.when((jm >= 0) & (jm < count))
        def _():
            h = own_head(jm)
            memory = dsuf_t[pl.ds(h, 1), :] * f_out[jm] + b_in[jm]
            m_out[jm] = memory
            memory_copy(jm).start()
            finish(h, e_own[jm], memory)

        @pl.when(it == 0)
        def _():
            for load in loads[2:]:
                load.wait()

        @pl.when(it < count)
        def _():
            for h in (own_head(it), other_head(it)):
                intra(q, k, v, cum_t, dintra, h)
                intra(pq, pk, pv, pcum_t, pintra, h)

        jr = it - 2 - last

        @pl.when((jr >= 0) & (jr < count))
        def _():
            entering_copy(jr).wait_recv()
            memory_copy(jr).wait_recv()
            finish(other_head(jr), e_in[jr], m_in[jr])

    squares = lax.dot_general(
        jnp.ones((8, hd), f32), acc[...], contract_lanes, precision=high, preferred_element_type=f32
    )
    sq[hx] = squares
    sq_copies = [
        pltpu.make_async_remote_copy(
            src_ref=sq.at[hx],
            dst_ref=sq.at[hx],
            send_sem=sq_send.at[i],
            recv_sem=sq_recv.at[i],
            device_id=peer,
            device_id_type=MESH,
        )
        for i, peer in enumerate(across)
    ]
    for copy in sq_copies:
        copy.start()
    for copy in sq_copies:
        copy.wait_recv()
    total = sq[0]
    for at in range(1, hn):
        total = total + sq[at]
    factor = lax.rsqrt(total / (hn * heads * hd) + epsilon)
    inside = lax.broadcasted_iota(jnp.int32, factor.shape, 1) < plen_ref[0]
    scale[...] = column(jnp.where(inside, factor, 0.0)[0:1], hd)

    @pl.loop(0, heads)
    def _(h):
        at = lanes_of(h)
        pob[:, at] = (pintra[h] * scale[...]).astype(pob.dtype)
        pltpu.make_async_copy(pob.at[:, at], pout_hbm.at[:, at], store_sem.at[1]).start()

    for copy in close_copies + sq_copies:
        copy.wait_send()

    @pl.loop(0, count)
    def _(j):
        state_copy(j).wait_send()
        entering_copy(j).wait_send()
        memory_copy(j).wait_send()

        @pl.when(c < n - 1)
        def _():
            forward_copy(j).wait_send()

        @pl.when(c > 0)
        def _():
            backward_copy(j).wait_send()

    pltpu.make_async_copy(dob, out_hbm, store_sem.at[0]).wait()
    pltpu.make_async_copy(pob, pout_hbm, store_sem.at[1]).wait()


def local(sizes, dq, dk, dv, dd, pq, pk, pv, pg, pd, plen, gain):
    n, hn, reps = sizes
    heads = dd.shape[1]
    rows, width = dq.shape
    hd = width // heads
    passages, prow = pq.shape[:2]
    assert passages == 1 and reps == 2 and heads % 2 == 0 and heads <= hd
    count = heads // 2
    f32, bf16 = jnp.float32, jnp.bfloat16
    pq, pk, pv, pg = (x.reshape(prow, width) for x in (pq, pk, pv, pg))
    anywhere = pl.BlockSpec(memory_space=pl.ANY)
    vmem = pl.BlockSpec(memory_space=pltpu.VMEM)
    smem = pl.BlockSpec(memory_space=pltpu.SMEM)
    blocks = n * reps
    chunks = pltpu.VMEM((count, hd, hd), f32)
    dma = pltpu.SemaphoreType.DMA
    out, pout = pl.pallas_call(
        functools.partial(kernel, n, hn, heads, hd),
        out_shape=(
            jax.ShapeDtypeStruct((rows, width), bf16),
            jax.ShapeDtypeStruct((prow, width), bf16),
        ),
        in_specs=[anywhere] * 3 + [vmem] + [anywhere] * 4 + [vmem, smem, vmem],
        out_specs=(anywhere, anywhere),
        scratch_shapes=[pltpu.VMEM((rows, width), bf16)] * 3
        + [pltpu.VMEM((prow, width), bf16)] * 4
        + [pltpu.VMEM((rows, width), bf16), pltpu.VMEM((prow, width), bf16)]
        + [pltpu.VMEM((heads, rows, hd), f32), pltpu.VMEM((heads, prow, hd), f32)]
        + [pltpu.VMEM((heads, rows), f32), pltpu.VMEM((heads, prow), f32)]
        + [pltpu.VMEM((blocks, 1, hd), f32)]
        + [pltpu.VMEM((hd, hd), f32)] * 3
        + [chunks] * 14
        + [pltpu.VMEM((prow, hd), f32), pltpu.VMEM((hn, 8, prow), f32), pltpu.VMEM((prow, hd), f32)]
        + [
            dma((7,)),
            dma((2,)),
            dma((blocks - 1,)),
            dma((blocks - 1,)),
            dma((3, count)),
            dma((3, count)),
            dma((2, count)),
            dma((2, count)),
            dma((max(hn - 1, 1),)),
            dma((max(hn - 1, 1),)),
        ],
        compiler_params=pltpu.CompilerParams(
            collective_id=0, has_side_effects=True, vmem_limit_bytes=60 << 20
        ),
    )(dq, dk, dv, dd, pq, pk, pv, pg, pd.reshape(prow, heads), plen, gain.reshape(1, width))
    return out, pout.reshape(passages, prow, width)


def solution(mesh):
    rows = ("groups", "seq", "rep")
    flat, deep = P(rows, "head"), P(rows, None, "head")
    sizes = tuple(mesh.shape[axis] for axis in ("seq", "head", "rep"))
    return jax.shard_map(
        functools.partial(local, sizes),
        mesh=mesh,
        in_specs=(flat,) * 4 + (deep,) * 5 + (P(rows), P("head")),
        out_specs=(flat, deep),
        check_vma=False,
    )
```

time: 283 us -> 68.5 us (0.24)
  waiting for transfers between devices: 165 us -> 0 us
  Pallas kernels: 0 us -> 59.3 us
  matrix products: 32.1 us -> 0 us
  other arithmetic: 24.6 us -> 0 us
  local copies, waits for them, and re-layouts: 26.6 us -> 7.63 us
  blocking collectives: 18.6 us -> 0 us
  between operations: 14.8 us -> 1.29 us
    all_gather x1 -> x0, waiting for transfers between devices: 128 us -> none  [entering_2(): everything = jax.tree.map(lambda part: lax.all_gather(part, axis), value)]
    pallas_call x0 -> x1, Pallas kernels: none -> 59.3 us  [local(): pl.pallas_call(functools.partial(kernel, n, hn, heads, hd), out_shape=(ja...]
    psum x1 -> x0, waiting for transfers between devices: 36.5 us -> none  [local(): memory = lax.psum(decay_after[:, None, None] * state_own, ('seq', 'rep'))]
    dot_general x5 -> x0, matrix products: 32.1 us -> none  [the longest x2 14 us: carried(): jnp.einsum('thd,hde->the', queries.astype(jnp.float32), state_full, preci...]
    select_n x16 -> x0, other arithmetic: 16.9 us -> none  [hop(): return jax.tree.map(lambda a, b: jnp.where(reached, a, b), new, before)]
    all_gather x1 -> x0, blocking collectives: 13.5 us -> none  [entering_2(): everything = jax.tree.map(lambda part: lax.all_gather(part, axis), value)]
    reshape x2 -> x0, local copies, waits for them, and re-layouts: 8.16 us -> none  [the longest x1 4.08 us: readout(): values_in.reshape(passage_rows, heads_here, head_dim)]
    broadcast_in_dim x1 -> x0, local copies, waits for them, and re-layouts: 6.07 us -> none  [local(): lax.map(readout, (passage_query, passage_key, passage_value, passage_decay))]
  transfers between devices with their start and end apart: 2 -> 0, of which waited for: 2 -> 0; matrix products, arithmetic and copies ran while one was open for 16% -> 0% of each run, Pallas kernels for 0% -> 0%
where the time goes in v1:
time: 68.5 us; the launch traced here: 68.3 us
  Pallas kernels  59.3 us (87%)
  local copies, waits for them, and re-layouts  7.63 us (11%)
  between operations  1.29 us (2%)
    pallas_call x1, Pallas kernels, local(): pl.pallas_call(functools.partial(kernel, n, hn, heads, hd), out_shape=(ja...  59.3 us
    unnamed x6, local copies, waits for them, and re-layouts  7.63 us

profile of v1, /device:TPU:0, one launch (start us, length us, event | category | flops | bytes accessed | tf_op | source)
XLA Modules:
  0.0 68.3 jit_solution(10662615584196952948)
XLA Ops:
  1.3 1.5 %copy.14.decay_ref = f32[256,32]{1,0:T(8,128)} copy(f32[256,32]{0,1:T(8,128)} %param.14) | data formatting | bytes 65536 | tf_op args[3]
  2.8 1.5 %copy.13 = f32[1,256,32]{2,1,0:T(8,128)} copy(f32[1,256,32]{1,2,0:T(8,128)} %param.19) | data formatting | bytes 65536 | tf_op args[8]
  4.3 59.3 %shard_map.122 = (bf16[256,4096]{1,0:T(8,128)(2,1)}, bf16[256,4096]{1,0:T(8,128)(2,1)}) custom-call(bf16[256,4096]{1,0:T(8,128)(2,1)} %q_hbm.1, bf16[256,4096]{1,0:T(8,128)(2,1)} %k_hbm.1, bf16[256,4096]{1,0:T(8,128)(2,1)} %v_hbm.1, f32[256,32]{1,0:T(8,128)} %copy.14.decay_ref, bf16[256,4096]{1,0:T(8,128)(2,1)} %bitcast.8, bf16[256,4096]{1,0:T(8,128)(2,1)} %bitcast.9, ...), custom_call_target="tpu_custom_call" | custom-call | tf_op jit(solution)/shard_map/pallas_call | solution.py:437
  63.6 0.0 copy-start
  63.7 3.3 %copy.18 = bf16[256,4096]{1,0:T(8,128)(2,1)} copy(bf16[256,4096]{1,0:T(8,128)(2,1)} %get-tuple-element.8) | data formatting | bytes 4194304
  66.9 0.0 copy-done
  66.9 1.3 %copy.19 = bf16[1,256,4096]{2,1,0:T(8,128)(2,1)} copy(bf16[1,256,4096]{2,1,0:T(8,128)(2,1)S(1)} %bitcast.7) | data formatting | bytes 4194304
Async XLA Ops:
  63.6 3.3 %copy-start = (bf16[256,4096]{1,0:T(8,128)(2,1)S(1)}, bf16[256,4096]{1,0:T(8,128)(2,1)}, u32[]{:S(2)}) copy-start(bf16[256,4096]{1,0:T(8,128)(2,1)} %get-tuple-element.5) | copy-start | bytes 6291460

commit v2 on v1

--- a/solution.py
+++ b/solution.py
@@ -8,7 +8,8 @@
 from jax.sharding import PartitionSpec as P
 
 epsilon = 1e-05
-LAG = 2
+LAG = 3
+AHEAD = 4
 MESH = pl.DeviceIdType.MESH
 
 
@@ -47,8 +48,8 @@
     pdecay_ref,
     plen_ref,
     gain_ref,
-    out_hbm,
-    pout_hbm,
+    dob,
+    pob,
     q,
     k,
     v,
@@ -56,8 +57,6 @@
     pk,
     pv,
     pg,
-    dob,
-    pob,
     dintra,
     pintra,
     cum_t,
@@ -84,7 +83,6 @@
     sq,
     scale,
     load_sem,
-    store_sem,
     close_send,
     close_recv,
     pair_send,
@@ -138,15 +136,13 @@
     contract_rows = (((0,), (0,)), ((), ()))
     contract_lanes = (((1,), (1,)), ((), ()))
     rates = decay_ref[...]
-    sums = jnp.dot(jnp.ones((8, rows), f32), rates, precision=high, preferred_element_type=f32)
+    sums = lax.dot_general(
+        jnp.ones((8, rows), f32), rates, contract_lanes, precision=high, preferred_element_type=f32
+    )
     closings[b] = jnp.zeros((1, hd), f32)
     closings[b, :, :heads] = sums[0:1]
-    cum_t[...] = lax.dot_general(
-        rates, upper(rows), contract_rows, precision=high, preferred_element_type=f32
-    )
-    pcum_t[...] = lax.dot_general(
-        pdecay_ref[...], upper(prow), contract_rows, precision=high, preferred_element_type=f32
-    )
+    cum_t[...] = jnp.dot(rates, upper(rows), precision=high, preferred_element_type=f32)
+    pcum_t[...] = jnp.dot(pdecay_ref[...], upper(prow), precision=high, preferred_element_type=f32)
     acc[...] = jnp.zeros_like(acc)
 
     @pl.when(c == 0)
@@ -254,22 +250,62 @@
         grow = column(jnp.exp(-cum_t[pl.ds(h, 1), :]), hd)
         at = lanes_of(h)
         dob[:, at] = (dintra[h] + grow * exact_dot(q[:, at], entering)).astype(dob.dtype)
-        pltpu.make_async_copy(dob.at[:, at], out_hbm.at[:, at], store_sem.at[0]).start()
         pgrow = column(jnp.exp(-pcum_t[pl.ds(h, 1), :]), hd)
         attended = pintra[h] + pgrow * exact_dot(pq[:, at], memory)
         acc[...] += attended * attended
         pintra[h] = attended * (gain_ref[:, at] * jax.nn.sigmoid(pg[:, at].astype(f32)))
 
-    last = jnp.maximum(c, n - 1 - c) * LAG
-
-    @pl.loop(0, count + (n - 1) * LAG + 2)
+    def combine(j):
+        state_copy(j).wait_recv()
+        one = jnp.where(r == 0, s_own[j], s_in[j])
+        two = jnp.where(r == 0, s_in[j], s_own[j])
+        s_first[j] = one
+        s_chip[j] = d1_t[pl.ds(own_head(j), 1), :] * one + two
+
+    def forward(j):
+        h = own_head(j)
+
+        @pl.when(c > 0)
+        def _():
+            forward_copy(j).wait_recv()
+
+        before = f_in[j]
+        d0, d1 = d0_t[pl.ds(h, 1), :], d1_t[pl.ds(h, 1), :]
+        f_out[j] = (d0 * d1) * before + s_chip[j]
+
+        @pl.when(c < n - 1)
+        def _():
+            forward_copy(j).start()
+
+        second = d0 * before + s_first[j]
+        e_own[j] = jnp.where(r == 0, before, second)
+        e_out[j] = jnp.where(r == 0, second, before)
+        entering_copy(j).start()
+
+    def backward(j):
+        @pl.when(c < n - 1)
+        def _():
+            backward_copy(j).wait_recv()
+
+        @pl.when(c > 0)
+        def _():
+            b_out[j] = dsuf_t[pl.ds(own_head(j), 1), :] * s_chip[j] + b_in[j]
+            backward_copy(j).start()
+
+    @pl.loop(0, count + AHEAD)
     def _(it):
         @pl.when(it == 0)
         def _():
             loads[0].wait()
             loads[1].wait()
 
-        @pl.when(it == 1)
+        @pl.when(it < count)
+        def _():
+            s_out[it] = state_of(other_head(it))
+            state_copy(it).start()
+            s_own[it] = state_of(own_head(it))
+
+        @pl.when(it == AHEAD)
         def _():
             for copy in close_copies:
                 copy.wait_recv()
@@ -284,59 +320,45 @@
             d1_t[...] = table(closings[2 * c + 1])
             dsuf_t[...] = table(later)
 
-        j0 = it - 1
-
-        @pl.when((j0 >= 0) & (j0 < count))
-        def _():
-            state_copy(j0).wait_recv()
-            one = jnp.where(r == 0, s_own[j0], s_in[j0])
-            two = jnp.where(r == 0, s_in[j0], s_own[j0])
-            s_first[j0] = one
-            s_chip[j0] = d1_t[pl.ds(own_head(j0), 1), :] * one + two
-
-        jf = it - 1 - c * LAG
-
-        @pl.when((jf >= 0) & (jf < count))
-        def _():
-            h = own_head(jf)
-
-            @pl.when(c > 0)
+        @pl.when(it >= AHEAD)
+        def _():
+            j = it - AHEAD
+            combine(j)
+
+            @pl.when(c == 0)
             def _():
-                forward_copy(jf).wait_recv()
-
-            before = f_in[jf]
-            d0, d1 = d0_t[pl.ds(h, 1), :], d1_t[pl.ds(h, 1), :]
-            f_out[jf] = (d0 * d1) * before + s_chip[jf]
-
-            @pl.when(c < n - 1)
+                forward(j)
+
+            @pl.when(c == n - 1)
             def _():
-                forward_copy(jf).start()
-
-            second = d0 * before + s_first[jf]
-            e_own[jf] = jnp.where(r == 0, before, second)
-            e_out[jf] = jnp.where(r == 0, second, before)
-            entering_copy(jf).start()
-
-        jb = it - 1 - (n - 1 - c) * LAG
-
-        @pl.when((jb >= 0) & (jb < count))
-        def _():
-            @pl.when(c < n - 1)
-            def _():
-                backward_copy(jb).wait_recv()
-
-            @pl.when(c > 0)
-            def _():
-                b_out[jb] = dsuf_t[pl.ds(own_head(jb), 1), :] * s_chip[jb] + b_in[jb]
-                backward_copy(jb).start()
+                backward(j)
+
+    for load in loads[2:]:
+        load.wait()
+
+    last = jnp.maximum(jnp.maximum(c - 1, n - 2 - c), 0) * LAG
+
+    @pl.loop(0, count + max(n - 2, 0) * LAG + 1)
+    def _(it):
+        jf = it - (c - 1) * LAG
+
+        @pl.when((c > 0) & (jf >= 0) & (jf < count))
+        def _():
+            forward(jf)
+
+        jb = it - (n - 2 - c) * LAG
+
+        @pl.when((c < n - 1) & (jb >= 0) & (jb < count))
+        def _():
+            backward(jb)
 
         @pl.when(it < count)
         def _():
-            s_out[it] = state_of(other_head(it))
-            state_copy(it).start()
-            s_own[it] = state_of(own_head(it))
-
-        jm = it - 1 - last
+            for h in (own_head(it), other_head(it)):
+                intra(q, k, v, cum_t, dintra, h)
+                intra(pq, pk, pv, pcum_t, pintra, h)
+
+        jm = it - last
 
         @pl.when((jm >= 0) & (jm < count))
         def _():
@@ -346,18 +368,7 @@
             memory_copy(jm).start()
             finish(h, e_own[jm], memory)
 
-        @pl.when(it == 0)
-        def _():
-            for load in loads[2:]:
-                load.wait()
-
-        @pl.when(it < count)
-        def _():
-            for h in (own_head(it), other_head(it)):
-                intra(q, k, v, cum_t, dintra, h)
-                intra(pq, pk, pv, pcum_t, pintra, h)
-
-        jr = it - 2 - last
+        jr = it - 1 - last
 
         @pl.when((jr >= 0) & (jr < count))
         def _():
@@ -395,7 +406,6 @@
     def _(h):
         at = lanes_of(h)
         pob[:, at] = (pintra[h] * scale[...]).astype(pob.dtype)
-        pltpu.make_async_copy(pob.at[:, at], pout_hbm.at[:, at], store_sem.at[1]).start()
 
     for copy in close_copies + sq_copies:
         copy.wait_send()
@@ -413,9 +423,6 @@
         @pl.when(c > 0)
         def _():
             backward_copy(j).wait_send()
-
-    pltpu.make_async_copy(dob, out_hbm, store_sem.at[0]).wait()
-    pltpu.make_async_copy(pob, pout_hbm, store_sem.at[1]).wait()
 
 
 def local(sizes, dq, dk, dv, dd, pq, pk, pv, pg, pd, plen, gain):
@@ -437,14 +444,13 @@
     out, pout = pl.pallas_call(
         functools.partial(kernel, n, hn, heads, hd),
         out_shape=(
-            jax.ShapeDtypeStruct((rows, width), bf16),
-            jax.ShapeDtypeStruct((prow, width), bf16),
+            pltpu.VMEM((rows, width), bf16),
+            pltpu.VMEM((prow, width), bf16),
         ),
         in_specs=[anywhere] * 3 + [vmem] + [anywhere] * 4 + [vmem, smem, vmem],
-        out_specs=(anywhere, anywhere),
+        out_specs=(vmem, vmem),
         scratch_shapes=[pltpu.VMEM((rows, width), bf16)] * 3
         + [pltpu.VMEM((prow, width), bf16)] * 4
-        + [pltpu.VMEM((rows, width), bf16), pltpu.VMEM((prow, width), bf16)]
         + [pltpu.VMEM((heads, rows, hd), f32), pltpu.VMEM((heads, prow, hd), f32)]
         + [pltpu.VMEM((heads, rows), f32), pltpu.VMEM((heads, prow), f32)]
         + [pltpu.VMEM((blocks, 1, hd), f32)]
@@ -453,7 +459,6 @@
         + [pltpu.VMEM((prow, hd), f32), pltpu.VMEM((hn, 8, prow), f32), pltpu.VMEM((prow, hd), f32)]
         + [
             dma((7,)),
-            dma((2,)),
             dma((blocks - 1,)),
             dma((blocks - 1,)),
             dma((3, count)),
@@ -464,9 +469,9 @@
             dma((max(hn - 1, 1),)),
         ],
         compiler_params=pltpu.CompilerParams(
-            collective_id=0, has_side_effects=True, vmem_limit_bytes=60 << 20
+            collective_id=0, has_side_effects=True, vmem_limit_bytes=50 << 20
         ),
-    )(dq, dk, dv, dd, pq, pk, pv, pg, pd.reshape(prow, heads), plen, gain.reshape(1, width))
+    )(dq, dk, dv, dd.T, pq, pk, pv, pg, pd.reshape(prow, heads).T, plen, gain.reshape(1, width))
     return out, pout.reshape(passages, prow, width)
 
 

time: 68.5 us -> 58.2 us (0.85)
  Pallas kernels: 59.3 us -> 54 us
  local copies, waits for them, and re-layouts: 7.63 us -> 2.64 us
    pallas_call x1, Pallas kernels: 59.3 us -> 54 us  [local(): pl.pallas_call(functools.partial(kernel, n, hn, heads, hd), out_shape=(pl...]
    unnamed x6 -> x2, local copies, waits for them, and re-layouts: 7.63 us -> 2.64 us
where the time goes in v2:
time: 58.2 us; the launch traced here: 57.9 us
  Pallas kernels  54 us (93%)
  local copies, waits for them, and re-layouts  2.64 us (5%)
  between operations  1.29 us (2%)
    pallas_call x1, Pallas kernels, local(): pl.pallas_call(functools.partial(kernel, n, hn, heads, hd), out_shape=(pl...  54 us
    unnamed x2, local copies, waits for them, and re-layouts  2.64 us

profile of v2, /device:TPU:0, one launch (start us, length us, event | category | flops | bytes accessed | tf_op | source)
XLA Modules:
  0.0 57.9 jit_solution(3660976183872265494)
XLA Ops:
  1.3 54.0 %shard_map.122 = (bf16[256,4096]{1,0:T(8,128)(2,1)S(1)}, bf16[256,4096]{1,0:T(8,128)(2,1)S(1)}) custom-call(bf16[256,4096]{1,0:T(8,128)(2,1)} %q_hbm.1, bf16[256,4096]{1,0:T(8,128)(2,1)} %k_hbm.1, bf16[256,4096]{1,0:T(8,128)(2,1)} %v_hbm.1, f32[32,256]{1,0:T(8,128)} %bitcast.15, bf16[256,4096]{1,0:T(8,128)(2,1)} %bitcast.11, bf16[256,4096]{1,0:T(8,128)(2,1)} %bitcast.12, ...), custom_call_target="tpu_custom_call" | custom-call | tf_op jit(solution)/shard_map/pallas_call | solution.py:444
  55.3 1.3 %copy.15 = bf16[256,4096]{1,0:T(8,128)(2,1)} copy(bf16[256,4096]{1,0:T(8,128)(2,1)S(1)} %get-tuple-element.6) | data formatting | bytes 4194304
  56.6 1.3 %copy.16 = bf16[1,256,4096]{2,1,0:T(8,128)(2,1)} copy(bf16[1,256,4096]{2,1,0:T(8,128)(2,1)S(1)} %bitcast.10) | data formatting | bytes 4194304

commit v3 on v2

--- a/solution.py
+++ b/solution.py
@@ -115,7 +115,7 @@
             ]
         )
     ]
-    for load in loads:
+    for load in loads[:2]:
         load.start()
 
     barrier = pltpu.get_barrier_semaphore()
@@ -298,6 +298,8 @@
         def _():
             loads[0].wait()
             loads[1].wait()
+            for load in loads[2:]:
+                load.start()
 
         @pl.when(it < count)
         def _():
@@ -352,29 +354,42 @@
         def _():
             backward(jb)
 
-        @pl.when(it < count)
-        def _():
+        jm = it - last
+
+        @pl.when((jm >= 0) & (jm < count))
+        def _():
+            m_out[jm] = dsuf_t[pl.ds(own_head(jm), 1), :] * f_out[jm] + b_in[jm]
+            memory_copy(jm).start()
+
+        def begin():
             for h in (own_head(it), other_head(it)):
                 intra(q, k, v, cum_t, dintra, h)
                 intra(pq, pk, pv, pcum_t, pintra, h)
 
-        jm = it - last
-
-        @pl.when((jm >= 0) & (jm < count))
-        def _():
-            h = own_head(jm)
-            memory = dsuf_t[pl.ds(h, 1), :] * f_out[jm] + b_in[jm]
-            m_out[jm] = memory
-            memory_copy(jm).start()
-            finish(h, e_own[jm], memory)
-
-        jr = it - 1 - last
-
-        @pl.when((jr >= 0) & (jr < count))
+        jr = jm - 1
+        ready = (jr >= 0) & (jr < count)
+
+        def end():
+            finish(own_head(jr), e_own[jr], m_out[jr])
+            finish(other_head(jr), e_in[jr], m_in[jr])
+
+        @pl.when(ready)
         def _():
             entering_copy(jr).wait_recv()
             memory_copy(jr).wait_recv()
-            finish(other_head(jr), e_in[jr], m_in[jr])
+
+        @pl.when((it < count) & jnp.logical_not(ready))
+        def _():
+            begin()
+
+        @pl.when((it < count) & ready)
+        def _():
+            end()
+            begin()
+
+        @pl.when((it >= count) & ready)
+        def _():
+            end()
 
     squares = lax.dot_general(
         jnp.ones((8, hd), f32), acc[...], contract_lanes, precision=high, preferred_element_type=f32

time: 58.2 us -> 56.1 us (0.964)
  Pallas kernels: 54 us -> 51.9 us
    pallas_call x1, Pallas kernels: 54 us -> 51.9 us  [local(): pl.pallas_call(functools.partial(kernel, n, hn, heads, hd), out_shape=(pl...]
where the time goes in v3:
time: 56.1 us; the launch traced here: 55.8 us
  Pallas kernels  51.9 us (93%)
  local copies, waits for them, and re-layouts  2.64 us (5%)
  between operations  1.29 us (2%)
    pallas_call x1, Pallas kernels, local(): pl.pallas_call(functools.partial(kernel, n, hn, heads, hd), out_shape=(pl...  51.9 us
    unnamed x2, local copies, waits for them, and re-layouts  2.64 us

profile of v3, /device:TPU:0, one launch (start us, length us, event | category | flops | bytes accessed | tf_op | source)
XLA Modules:
  0.0 55.8 jit_solution(6995962457895542753)
XLA Ops:
  1.3 51.9 %shard_map.122 = (bf16[256,4096]{1,0:T(8,128)(2,1)S(1)}, bf16[256,4096]{1,0:T(8,128)(2,1)S(1)}) custom-call(bf16[256,4096]{1,0:T(8,128)(2,1)} %q_hbm.1, bf16[256,4096]{1,0:T(8,128)(2,1)} %k_hbm.1, bf16[256,4096]{1,0:T(8,128)(2,1)} %v_hbm.1, f32[32,256]{1,0:T(8,128)} %bitcast.15, bf16[256,4096]{1,0:T(8,128)(2,1)} %bitcast.11, bf16[256,4096]{1,0:T(8,128)(2,1)} %bitcast.12, ...), custom_call_target="tpu_custom_call" | custom-call | tf_op jit(solution)/shard_map/pallas_call | solution.py:459
  53.2 1.3 %copy.15 = bf16[256,4096]{1,0:T(8,128)(2,1)} copy(bf16[256,4096]{1,0:T(8,128)(2,1)S(1)} %get-tuple-element.6) | data formatting | bytes 4194304
  54.5 1.3 %copy.16 = bf16[1,256,4096]{2,1,0:T(8,128)(2,1)} copy(bf16[1,256,4096]{2,1,0:T(8,128)(2,1)S(1)} %bitcast.10) | data formatting | bytes 4194304
